TPU v7x, 32 devices: a whole 2x2x4 slice. The times are simulated.
32 devices in a mesh: ad: 8 (over z, core), tp: 4 (over y, x).
Axes of the slice: x: 2, y: 2, z: 4, core: 2. Of those that a mesh axis runs over, the one named last changes fastest.
Arguments:
- tokens: bfloat16 [1024, 8192], P('ad', 'tp'), may hold values from -6 to 6
- query_weight: bfloat16 [8192, 8192], P(None, 'tp'), may hold values from -0.0625 to 0.0625
- adapter_down_weight: bfloat16 [128, 8192, 64], P('ad', 'tp'), may hold values from -0.0625 to 0.0625
- adapter_up_weight: bfloat16 [128, 64, 8192], P('ad', None, 'tp'), may hold values from -0.75 to 0.75
- row_adapter_index: int32 [1024], P('ad'), may hold values from 0 to 127, as said below
- adapter_table_slot: int32 [128], replicated, may hold values from 0 to 127, as said below
- lengths: int32 [1024], P('ad'), may hold values from 1 to 64, as said below
- cached_key_rows: bfloat16 [1024, 8, 64, 128], P('ad', None, 'tp'), may hold values from -360 to 360
- cached_value_rows: bfloat16 [1024, 8, 64, 128], P('ad', None, 'tp'), may hold values from -6 to 6
Outputs:
- queries: bfloat16 [1024, 8192], P('ad', 'tp')
- attended: bfloat16 [1024, 8192], P('ad', 'tp')
Inputs may be any that keep to these rules, and one draw needn't show every extreme that they name: `row_adapter_index`: within each aligned block of 128 rows at most 48 rows have their adapter's slot in any one run of 16 slots (slot // 16); one such run, drawn from the seed, is named by exactly 48 rows of every block. `adapter_table_slot`: A permutation of the slots. `lengths`: some row has exactly 64 and some row exactly 1.
All inputs are finite; a program needn't handle non-finite values.
Results may differ from a plain program's by a relative error of at most 0.019.
Values may be sent and summed in bfloat16 or wider, within the bound.
A program may use at most 128 MiB of HBM per device.

v0:
```python
import math
import jax
import jax.numpy as jnp
from jax import lax
from jax.sharding import PartitionSpec as P


def rotate(query, lengths):
    head_dim = query.shape[-1]
    half = head_dim // 2
    freq = jnp.exp(jnp.arange(half, dtype=jnp.float32) * (-2.0 * math.log(500000.0) / head_dim))
    angle = (lengths - 1).astype(jnp.float32)[:, None, None] * freq[None, None, :]
    cosine = jnp.cos(angle)
    sine = jnp.sin(angle)
    first = query[..., :half]
    second = query[..., half:]
    return jnp.concatenate(
        [first * cosine - second * sine, second * cosine + first * sine], axis=-1
    )


def lookup(ids, adapter_table_slot):
    table = jnp.arange(adapter_table_slot.shape[0], dtype=jnp.int32)
    return jnp.sum(
        jnp.where(ids[:, None] == table[None, :], adapter_table_slot[None, :], 0), axis=1
    )


def shrink_rows(input_rows, local_partial, adapter_down_weight):
    adapter_row_count = adapter_down_weight.shape[0]
    select_rows = (
        local_partial[:, None] == jnp.arange(adapter_row_count, dtype=jnp.int32)[None, :]
    ).astype(jnp.float32)
    update_terms = jnp.einsum(
        "nt,vtm->nvm", input_rows, adapter_down_weight, preferred_element_type=jnp.float32
    )
    return (select_rows, jnp.sum(update_terms * select_rows[:, :, None], axis=1))


def expand_rows(select_rows, reduced_rows, adapter_up_weight):
    spread_rows = (select_rows[:, :, None] * reduced_rows.astype(jnp.float32)[:, None, :]).astype(
        jnp.bfloat16
    )
    return jnp.einsum(
        "pow,owu->pu", spread_rows, adapter_up_weight, preferred_element_type=jnp.float32
    ).astype(jnp.bfloat16)


def per_device(
    tokens,
    query_weight,
    adapter_down_weight,
    adapter_up_weight,
    row_adapter_index,
    adapter_table_slot,
    lengths,
    cached_key_rows,
    cached_value_rows,
):
    rows = tokens.shape[0]
    columns = query_weight.shape[1]
    tp_count = lax.axis_size("tp")
    owner_partials = adapter_down_weight.shape[0]
    base = jnp.dot(
        lax.all_gather(tokens, "tp", axis=1, tiled=True),
        query_weight,
        preferred_element_type=jnp.float32,
    )
    combined_output, every_id = (
        lax.all_gather(tokens, "ad", axis=0, tiled=True),
        lax.all_gather(row_adapter_index, "ad", axis=0, tiled=True),
    )
    slots = lookup(every_id, adapter_table_slot)
    mine = slots // owner_partials == lax.axis_index("ad")
    local_partial = jnp.where(mine, slots % owner_partials, -1)
    select_rows, partial_value_sum = shrink_rows(
        combined_output, local_partial, adapter_down_weight
    )
    reduced_rows = lax.psum(partial_value_sum, "tp").astype(jnp.bfloat16)
    lowrank_change = expand_rows(select_rows, reduced_rows, adapter_up_weight)
    delta = lax.psum_scatter(
        lowrank_change.astype(jnp.float32).astype(jnp.bfloat16),
        "ad",
        scatter_dimension=0,
        tiled=True,
    ).astype(jnp.float32)
    head_dim = cached_key_rows.shape[3]
    query = (base + delta).reshape(rows, columns // head_dim, head_dim)
    queries = rotate(query, lengths).reshape(rows, columns).astype(jnp.bfloat16)
    every_head = lax.all_gather(queries, "tp", axis=1, tiled=True)
    kv_heads = cached_key_rows.shape[1]
    span = cached_key_rows.shape[2]
    grouped = every_head.reshape(rows, kv_heads, -1, head_dim)
    scores = jnp.einsum(
        "rkgd,rkpd->rkgp", grouped, cached_key_rows, preferred_element_type=jnp.float32
    ) * (1.0 / math.sqrt(head_dim))
    position = lax.axis_index("tp") * span + jnp.arange(span, dtype=jnp.int32)
    valid = (position[None, :] < lengths[:, None])[:, None, None, :]
    scores = jnp.where(valid, scores, -1e30)
    peak = jnp.max(scores, axis=-1)
    weights = jnp.where(valid, jnp.exp(scores - peak[..., None]), 0.0)
    total = jnp.sum(weights, axis=-1)
    partial_out = jnp.einsum(
        "rkgp,rkpd->rkgd",
        weights.astype(jnp.bfloat16),
        cached_value_rows,
        preferred_element_type=jnp.float32,
    ).astype(jnp.bfloat16)
    peaks, totals = (
        lax.all_to_all(
            peak.reshape(rows, tp_count, -1), "tp", split_axis=1, concat_axis=1, tiled=True
        ),
        lax.all_to_all(
            total.reshape(rows, tp_count, -1), "tp", split_axis=1, concat_axis=1, tiled=True
        ),
    )
    partials = lax.all_to_all(
        partial_out.reshape(rows, tp_count, -1), "tp", split_axis=1, concat_axis=1, tiled=True
    )
    highest = jnp.max(peaks, axis=1, keepdims=True)
    factor = jnp.exp(peaks - highest)
    numer = jnp.sum(
        factor[..., None] * partials.reshape(rows, tp_count, -1, head_dim).astype(jnp.float32),
        axis=1,
    )
    denom = jnp.sum(factor * totals, axis=1)
    attended = (numer / denom[..., None]).reshape(rows, columns).astype(jnp.bfloat16)
    return (queries, attended)


def solution(mesh):
    return jax.shard_map(
        per_device,
        mesh=mesh,
        in_specs=(
            P("ad", "tp"),
            P(None, "tp"),
            P("ad", "tp", None),
            P("ad", None, "tp"),
            P("ad"),
            P(),
            P("ad"),
            P("ad", None, "tp", None),
            P("ad", None, "tp", None),
        ),
        out_specs=(P("ad", "tp"), P("ad", "tp")),
        check_vma=False,
    )
```

profile of v0, /device:TPU:0, one launch (start us, length us, event | category | flops | bytes accessed | tf_op | source)
XLA Modules:
  0.0 274.9 jit_solution(6826846657034868188)
XLA Ops:
  7.2 0.0 all-gather.7.cloned.1.call-start
  7.2 0.7 all-gather.7.cloned.1.call-update
  7.9 0.0 all-gather.5.cloned.1.call-start
  7.9 0.7 all-gather.5.cloned.1.call-update
  8.6 0.0 reduce-scatter.2.cloned.1.call-start
  8.7 13.5 %all-gather = s32[8,1,128]{2,1,0:T(1,128)S(1)} all-gather(s32[1,1,128]{2,1,0:T(1,128)} %bitcast.48), channel_id=1, replica_groups=mesh['ad'=8,'tp'=4] {'ad'}, dimensions={0}, use_global_device_ids=true | all-gather | bytes 4608 | tf_op jit(solution)/shard_map/all_gather | solution.py:71
  22.2 1.0 select_reduce_fusion
  23.3 36.2 %all-gather.7.cloned.1.call-done = bf16[1024,2048]{1,0:T(8,128)(2,1)} async-done(((bf16[128,2048]{1,0:T(8,128)(2,1)}), bf16[1024,2048]{1,0:T(8,128)(2,1)}) %all-gather.7.cloned.1.call-update) | async-done | bytes 4194320 | tf_op jit(solution)/shard_map/all_gather | solution.py:70
  59.5 7.6 %fusion.25 = f32[1024,1024]{0,1:S(1)} fusion(bf16[1024,2048]{1,0:T(8,128)(2,1)} %all-gather.7.cloned.1.call-done, bf16[2048,1024]{0,1:T(8,128)(2,1)} %bitcast.49), kind=kOutput, calls=%fused_computation.52 | convolution fusion | flops 4294967296 | bytes 12582912
  67.1 0.6 multiply_reduce_fusion.1
  67.6 25.3 %all-reduce.1 = bf16[1024,64]{0,1:T(8,128)(2,1)S(1)} all-reduce(f32[1024,64]{0,1:T(8,128)S(1)} %multiply_reduce_fusion.1), channel_id=1, replica_groups=mesh['ad'=8,'tp'=4] {'tp'}, use_global_device_ids=true, to_apply=%region_2.3 | all-reduce | flops 65536 | bytes 393216 | tf_op jit(solution)/shard_map/psum | solution.py:79
  93.0 8.3 %bitcast_convert_fusion = bf16[1024,2048]{1,0:T(8,128)(2,1)} fusion(bf16[16,64,2048]{2,1,0:T(8,128)(2,1)} %param.12, f32[1024,64]{0,1:T(8,128)S(1)} %convert_element_type.71, f32[1024,16]{0,1:T(8,128)S(1)} %fusion.17), kind=kOutput, calls=%fused_computation | convolution fusion | flops 4299161600 | bytes 8716288 | tf_op jit(solution)/shard_map/pow,owu->pu/dot_general | solution.py:44
  101.3 0.0 copy-start.1
  101.3 0.0 reduce-scatter.2.cloned.1.call-update
  101.3 0.2 all-gather.9.cloned.1.call-start
  101.5 0.4 copy-done.1
  101.9 0.3 multiply_cosine_fusion
  102.2 0.0 all-gather.5.cloned.1.call-done
  102.3 49.9 %reduce-scatter.2.cloned.1.call-done = bf16[128,2048]{1,0:T(8,128)(2,1)} async-done(((bf16[1024,2048]{1,0:T(8,128)(2,1)}), bf16[128,2048]{1,0:T(8,128)(2,1)}) %reduce-scatter.2.cloned.1.call-update) | async-done | bytes 524304 | tf_op jit(solution)/shard_map/reduce_scatter | solution.py:81
  152.1 15.7 %fusion.15 = f32[16,8,16,128]{3,1,2,0:T(8,128)S(1)} fusion(bf16[128,8192]{1,0:T(8,128)(2,1)} %all-gather.5.cloned.1.call-done, bf16[8192,2048]{1,0:T(8,128)(2,1)} %param.10, bf16[128,2048]{1,0:T(8,128)(2,1)} %reduce-scatter.2.cloned.1.call-done), kind=kOutput, calls=%fused_computation.19 | convolution fusion | flops 4295491584 | bytes 37224448 | tf_op jit(solution)/shard_map/dot_general | solution.py:64
  167.8 0.2 copy.23
  168.0 0.5 subtract_convert_fusion
  168.6 0.3 pad_maximum_fusion
  168.9 0.9 copy.29
  169.8 0.0 all-gather.9.cloned.1.call-update
  169.8 0.1 broadcast_compare_fusion
  169.9 33.5 %all-gather.9.cloned.1.call-done = bf16[128,8192]{1,0:T(8,128)(2,1)} async-done(((bf16[128,2048]{1,0:T(8,128)(2,1)}), bf16[128,8192]{1,0:T(8,128)(2,1)}) %all-gather.9.cloned.1.call-update) | async-done | bytes 2097168 | tf_op jit(solution)/shard_map/all_gather | solution.py:90
  203.4 0.0 copy-start
  203.4 2.3 copy.25
  205.8 0.5 copy-done
  206.3 4.2 %fusion = (f32[128,8,8]{2,1,0:T(8,128)S(1)}, f32[128,8,8,16]{3,2,1,0:T(8,128)}) fusion(pred[128,16]{1,0:T(8,128)(4,1)S(1)} %broadcast_compare_fusion, bf16[128,8,8,128]{3,2,1,0:T(8,128)(2,1)S(1)} %bitcast.40, bf16[128,8,16,128]{3,2,1,0:T(8,128)(2,1)S(1)} %copy-done), kind=kOutput, calls=%fused_computation.6 | convolution fusion | flops 33939456 | bytes 6850560 | tf_op jit(solution)/shard_map/rkgd,rkpd->rkgp/dot_general | solution.py:94
  210.5 0.8 copy.18
  211.3 3.3 %all-to-all-start = ((f32[128,4,16]{0,2,1:T(8,128)}), f32[128,4,16]{0,2,1:T(8,128)S(1)}, u32[]{:S(2)}, u32[]{:S(2)}) async-start(f32[128,4,16]{0,2,1:T(8,128)} %bitcast.6), calls=%async_computation.1 | async-start | bytes 65536 | tf_op jit(solution)/shard_map/all_to_all | solution.py:110
  214.6 4.7 %fusion.1 = f32[128,8,8]{2,1,0:T(8,128)S(1)} fusion(f32[128,8,8,16]{3,2,1,0:T(8,128)} %get-tuple-element.9, f32[128,8,8]{2,1,0:T(8,128)S(1)} %get-tuple-element.8, pred[128,16]{1,0:T(8,128)(4,1)S(1)} %broadcast_compare_fusion), kind=kLoop, calls=%fused_computation.7 | loop fusion | flops 647168 | bytes 591872 | tf_op jit(solution)/shard_map/reduce_sum | solution.py:102
  219.3 0.8 copy.21
  220.1 0.0 all-to-all-done
  220.1 4.2 %all-to-all-start.2 = ((f32[128,4,16]{0,2,1:T(8,128)}), f32[128,4,16]{0,2,1:T(8,128)S(1)}, u32[]{:S(2)}, u32[]{:S(2)}) async-start(f32[128,4,16]{0,2,1:T(8,128)} %bitcast.7), calls=%async_computation.3 | async-start | bytes 65536 | tf_op jit(solution)/shard_map/all_to_all | solution.py:113
  224.3 6.4 %fusion.12 = bf16[128,8,8,128]{3,2,1,0:T(8,128)(2,1)} fusion(bf16[128,8,16,128]{3,2,1,0:T(8,128)(2,1)} %param.17, f32[128,8,8,16]{3,2,1,0:T(8,128)} %get-tuple-element.9, f32[128,8,8]{2,1,0:T(8,128)S(1)} %get-tuple-element.8, pred[128,16]{1,0:T(8,128)(4,1)S(1)} %broadcast_compare_fusion), kind=kOutput, calls=%fused_computation.18 | convolution fusion | flops 35258368 | bytes 6850560 | tf_op jit(solution)/shard_map/rkgp,rkpd->rkgd/dot_general | solution.py:103
  230.6 2.5 reshape.175
  233.2 2.5 copy.20
  235.7 0.0 all-to-all-done.2
  235.7 4.2 %all-to-all-start.1 = ((bf16[128,4,2048]{2,0,1:T(8,128)(2,1)}), bf16[128,4,2048]{2,0,1:T(8,128)(2,1)S(1)}, u32[]{:S(2)}, u32[]{:S(2)}) async-start(bf16[128,4,2048]{2,0,1:T(8,128)(2,1)} %copy.20), calls=%async_computation.2 | async-start | bytes 4194304 | tf_op jit(solution)/shard_map/all_to_all | solution.py:117
  240.0 0.1 copy.22
  240.1 0.1 copy.19
  240.2 2.6 mul.119
  242.8 4.9 %mul.120 = f32[128,4,2048]{2,0,1:T(8,128)} reshape(f32[128,4,16,128]{3,2,0,1:T(8,128)} %mul.119) | data formatting | bytes 8388608 | tf_op jit(solution)/shard_map/mul | solution.py:123
  247.7 16.3 %all-to-all-done.1 = bf16[128,4,2048]{2,0,1:T(8,128)(2,1)S(1)} async-done(((bf16[128,4,2048]{2,0,1:T(8,128)(2,1)}), bf16[128,4,2048]{2,0,1:T(8,128)(2,1)S(1)}, u32[]{:S(2)}, u32[]{:S(2)}) %all-to-all-start.1) | async-done | bytes 2097184 | tf_op jit(solution)/shard_map/all_to_all | solution.py:117
  264.0 2.9 %multiply_reduce_fusion = f32[128,2048]{1,0:T(8,128)S(1)} fusion(f32[128,4,2048]{2,0,1:T(8,128)} %mul.120, bf16[128,4,2048]{2,0,1:T(8,128)(2,1)S(1)} %all-to-all-done.1), kind=kLoop, calls=%fused_computation.1 | loop fusion | flops 2883584 | bytes 7340032 | tf_op jit(solution)/shard_map/reduce_sum | solution.py:122
  266.9 0.3 div.27
  267.2 1.2 fusion.16
  (8 shorter events, 0.1 us)
Async XLA Ops:
  7.2 52.3 %all-gather.7.cloned.1.call-start = ((), (), s32[]{:S(2)}) async-start(), calls=%async_computation.5 | async-start | bytes 4718592 | tf_op jit(solution)/shard_map/all_gather | solution.py:70
  7.9 94.4 %all-gather.5.cloned.1.call-start = ((), (), s32[]{:S(2)}) async-start(), calls=%async_computation.4 | async-start | bytes 2621440 | tf_op jit(solution)/shard_map/all_gather | solution.py:65
  8.6 143.5 %reduce-scatter.2.cloned.1.call-start = ((), (), s32[]{:S(2)}) async-start(), calls=%async_computation.6 | async-start | bytes 4718592 | tf_op jit(solution)/shard_map/reduce_scatter | solution.py:81
  101.3 0.7 copy-start.1
  101.3 102.1 %all-gather.9.cloned.1.call-start = ((), (), s32[]{:S(2)}) async-start(), calls=%async_computation.7 | async-start | bytes 2621440 | tf_op jit(solution)/shard_map/all_gather | solution.py:90
  203.4 2.8 %copy-start = (bf16[128,8,16,128]{3,2,1,0:T(8,128)(2,1)S(1)}, bf16[128,8,16,128]{3,2,1,0:T(8,128)(2,1)}, u32[]{:S(2)}) copy-start(bf16[128,8,16,128]{3,2,1,0:T(8,128)(2,1)} %param.16) | copy-start | bytes 12582916
  211.3 8.8 %all-to-all-start = ((f32[128,4,16]{0,2,1:T(8,128)}), f32[128,4,16]{0,2,1:T(8,128)S(1)}, u32[]{:S(2)}, u32[]{:S(2)}) async-start(f32[128,4,16]{0,2,1:T(8,128)} %bitcast.6), calls=%async_computation.1 | async-start | bytes 65536 | tf_op jit(solution)/shard_map/all_to_all | solution.py:110
  220.1 15.6 %all-to-all-start.2 = ((f32[128,4,16]{0,2,1:T(8,128)}), f32[128,4,16]{0,2,1:T(8,128)S(1)}, u32[]{:S(2)}, u32[]{:S(2)}) async-start(f32[128,4,16]{0,2,1:T(8,128)} %bitcast.7), calls=%async_computation.3 | async-start | bytes 65536 | tf_op jit(solution)/shard_map/all_to_all | solution.py:113
  235.7 28.2 %all-to-all-start.1 = ((bf16[128,4,2048]{2,0,1:T(8,128)(2,1)}), bf16[128,4,2048]{2,0,1:T(8,128)(2,1)S(1)}, u32[]{:S(2)}, u32[]{:S(2)}) async-start(bf16[128,4,2048]{2,0,1:T(8,128)(2,1)} %copy.20), calls=%async_computation.2 | async-start | bytes 4194304 | tf_op jit(solution)/shard_map/all_to_all | solution.py:117
Sparse Core Ops, SparseCore 0:
  9.6 49.8 all-gather.6
  61.3 38.7 all-gather.4
  102.4 49.6 reduce-scatter.1
  169.9 33.4 all-gather.8
where the time goes:
time: 276 us; the launch traced here: 275 us
  waiting for transfers between devices  137 us (50%)
  matrix products  42.2 us (15%)
  blocking collectives  38.9 us (14%)
  local copies, waits for them, and re-layouts  19 us (7%)
  between operations  13.9 us (5%)
  starting transfers between devices  11.9 us (4%)
  other arithmetic  11.7 us (4%)
    reduce_scatter x1, waiting for transfers between devices, per_device(): lax.psum_scatter(lowrank_change.astype(jnp.float32).astype(jnp.bfloat16),...  49.9 us
    all_gather x1, waiting for transfers between devices, per_device(): lax.all_gather(tokens, 'ad', axis=0, tiled=True)  36.2 us
    all_gather x1, waiting for transfers between devices, per_device(): every_head = lax.all_gather(queries, 'tp', axis=1, tiled=True)  33.5 us
    psum x1, blocking collectives, per_device(): reduced_rows = lax.psum(partial_value_sum, 'tp').astype(jnp.bfloat16)  25.3 us
    all_to_all x1, waiting for transfers between devices, per_device(): lax.all_to_all(partial_out.reshape(rows, tp_count, -1), 'tp', split_axis=...  16.3 us
    dot_general x1, matrix products, per_device(): jnp.dot(lax.all_gather(tokens, 'tp', axis=1, tiled=True), query_weight, p...  15.7 us
    all_gather x1, blocking collectives, per_device(): lax.all_gather(row_adapter_index, 'ad', axis=0, tiled=True)  13.5 us
    dot_general x1, matrix products, expand_rows(): jnp.einsum('pow,owu->pu', spread_rows, adapter_up_weight, preferred_eleme...  8.29 us
  transfers between devices with their start and end apart: 7, of which 4 were waited for; matrix products, arithmetic and copies ran while one was open for 15% of the time, Pallas kernels for 0%

commit v1 on v0

--- a/solution.py
+++ b/solution.py
@@ -1,8 +1,36 @@
+import functools
 import math
 import jax
 import jax.numpy as jnp
 from jax import lax
 from jax.sharding import PartitionSpec as P
+
+
+def tell_copies(panel, row_dim):
+    prior = lax.axis_size("tp")
+    view_out = lax.axis_index("tp")
+    odd, mat_out, reply = (prior, view_out, panel.shape[row_dim])
+    pages = [ix * odd if j0 == row_dim else ix for j0, ix in enumerate(panel.shape)]
+    wide_out = jnp.zeros(pages, panel.dtype)
+    block_last = lax.dynamic_update_slice_in_dim(wide_out, panel, mat_out * reply, axis=row_dim)
+    main = response = panel
+    for kk in range(1, odd // 2 + 1):
+        step_out = range(odd)
+        arr_now = map(lambda j0: (j0, (j0 + 1) % odd), step_out)
+        main = lax.ppermute(main, axis_name="tp", perm=list(arr_now))
+        block_last = lax.dynamic_update_slice_in_dim(
+            block_last, main, (mat_out - kk) % odd * reply, axis=row_dim
+        )
+        if 2 * kk < odd:
+            outcome_arr = list(map(lambda j0: (j0, (j0 - 1) % odd), range(odd)))
+            response = lax.ppermute(response, axis_name="tp", perm=outcome_arr)
+            block_last = lax.dynamic_update_slice_in_dim(
+                block_last, response, (mat_out + kk) % odd * reply, axis=row_dim
+            )
+    return block_last
+
+
+pair_links_up = functools.partial(tell_copies, row_dim=1)
 
 
 def rotate(query, lengths):
@@ -87,7 +115,7 @@
     head_dim = cached_key_rows.shape[3]
     query = (base + delta).reshape(rows, columns // head_dim, head_dim)
     queries = rotate(query, lengths).reshape(rows, columns).astype(jnp.bfloat16)
-    every_head = lax.all_gather(queries, "tp", axis=1, tiled=True)
+    every_head = pair_links_up(queries)
     kv_heads = cached_key_rows.shape[1]
     span = cached_key_rows.shape[2]
     grouped = every_head.reshape(rows, kv_heads, -1, head_dim)

time: 276 us -> 275 us (level)
  waiting for transfers between devices: 137 us -> 134 us
    all_gather x1 -> x0, waiting for transfers between devices: 33.5 us -> none  [per_device(): every_head = lax.all_gather(queries, 'tp', axis=1, tiled=True)]
    ppermute x0 -> x3, waiting for transfers between devices: none -> 30.2 us  [the longest x2 19.6 us: tell_copies(): main = lax.ppermute(main, axis_name='tp', perm=list(arr_now))]
    all_to_all x1, waiting for transfers between devices: 0.01 us -> 3.91 us  [per_device(): lax.all_to_all(total.reshape(rows, tp_count, -1), 'tp', split_axis=1, con...]
    all_to_all x1, waiting for transfers between devices: 16.3 us -> 12.6 us  [per_device(): lax.all_to_all(partial_out.reshape(rows, tp_count, -1), 'tp', split_axis=...]
    ppermute x0 -> x3, starting transfers between devices: none -> 3.53 us  [the longest x2 2.05 us: tell_copies(): main = lax.ppermute(main, axis_name='tp', perm=list(arr_now))]
  transfers between devices with their start and end apart: 7 -> 9, of which waited for: 4 -> 7; matrix products, arithmetic and copies ran while one was open for 15% -> 14% of each run, Pallas kernels for 0% -> 0%
where the time goes in v1:
time: 275 us; the launch traced here: 272 us
  waiting for transfers between devices  134 us (49%)
  matrix products  40.3 us (15%)
  blocking collectives  39 us (14%)
  local copies, waits for them, and re-layouts  20.6 us (7%)
  starting transfers between devices  14.3 us (5%)
  between operations  14.1 us (5%)
  other arithmetic  10 us (4%)
    reduce_scatter x1, waiting for transfers between devices, per_device(): lax.psum_scatter(lowrank_change.astype(jnp.float32).astype(jnp.bfloat16),...  49.6 us
    all_gather x1, waiting for transfers between devices, per_device(): lax.all_gather(tokens, 'ad', axis=0, tiled=True)  36.2 us
    psum x1, blocking collectives, per_device(): reduced_rows = lax.psum(partial_value_sum, 'tp').astype(jnp.bfloat16)  25.5 us
    ppermute x2, waiting for transfers between devices, tell_copies(): main = lax.ppermute(main, axis_name='tp', perm=list(arr_now))  19.6 us
    dot_general x1, matrix products, per_device(): jnp.dot(lax.all_gather(tokens, 'tp', axis=1, tiled=True), query_weight, p...  15.7 us
    all_gather x1, blocking collectives, per_device(): lax.all_gather(row_adapter_index, 'ad', axis=0, tiled=True)  13.5 us
    all_to_all x1, waiting for transfers between devices, per_device(): lax.all_to_all(partial_out.reshape(rows, tp_count, -1), 'tp', split_axis=...  12.6 us
    ppermute x1, waiting for transfers between devices, tell_copies(): response = lax.ppermute(response, axis_name='tp', perm=outcome_arr)  10.6 us
  transfers between devices with their start and end apart: 9, of which 7 were waited for; matrix products, arithmetic and copies ran while one was open for 14% of the time, Pallas kernels for 0%

profile of v1, /device:TPU:0, one launch (start us, length us, event | category | flops | bytes accessed | tf_op | source)
XLA Modules:
  0.0 272.2 jit_solution(11745062555348634196)
XLA Ops:
  7.2 0.0 all-gather.6.cloned.1.call-start
  7.2 0.7 all-gather.6.cloned.1.call-update
  7.9 0.0 all-gather.4.cloned.1.call-start
  7.9 0.7 all-gather.4.cloned.1.call-update
  8.6 0.0 reduce-scatter.2.cloned.1.call-start
  8.7 13.5 %all-gather = s32[8,1,128]{2,1,0:T(1,128)S(1)} all-gather(s32[1,1,128]{2,1,0:T(1,128)} %bitcast.46), channel_id=1, replica_groups=mesh['ad'=8,'tp'=4] {'ad'}, dimensions={0}, use_global_device_ids=true | all-gather | bytes 4608 | tf_op jit(solution)/shard_map/all_gather | solution.py:99
  22.2 1.0 select_reduce_fusion
  23.3 36.2 %all-gather.6.cloned.1.call-done = bf16[1024,2048]{1,0:T(8,128)(2,1)} async-done(((bf16[128,2048]{1,0:T(8,128)(2,1)}), bf16[1024,2048]{1,0:T(8,128)(2,1)}) %all-gather.6.cloned.1.call-update) | async-done | bytes 4194320 | tf_op jit(solution)/shard_map/all_gather | solution.py:98
  59.5 7.6 %fusion.25 = f32[1024,1024]{0,1:S(1)} fusion(bf16[1024,2048]{1,0:T(8,128)(2,1)} %all-gather.6.cloned.1.call-done, bf16[2048,1024]{0,1:T(8,128)(2,1)} %bitcast.47), kind=kOutput, calls=%fused_computation.56 | convolution fusion | flops 4294967296 | bytes 12582912
  67.1 0.6 multiply_reduce_fusion.1
  67.6 25.5 %all-reduce.1 = bf16[1024,64]{0,1:T(8,128)(2,1)S(1)} all-reduce(f32[1024,64]{0,1:T(8,128)S(1)} %multiply_reduce_fusion.1), channel_id=1, replica_groups=mesh['ad'=8,'tp'=4] {'tp'}, use_global_device_ids=true, to_apply=%region_2.3 | all-reduce | flops 65536 | bytes 393216 | tf_op jit(solution)/shard_map/psum | solution.py:107
  93.1 8.3 %bitcast_convert_fusion = bf16[1024,2048]{1,0:T(8,128)(2,1)} fusion(bf16[16,64,2048]{2,1,0:T(8,128)(2,1)} %param.12, f32[1024,64]{0,1:T(8,128)S(1)} %convert_element_type.71, f32[1024,16]{0,1:T(8,128)S(1)} %fusion.17), kind=kOutput, calls=%fused_computation | convolution fusion | flops 4299161600 | bytes 8716288 | tf_op jit(solution)/shard_map/pow,owu->pu/dot_general | solution.py:72
  101.4 0.0 copy-start.3
  101.4 0.0 reduce-scatter.2.cloned.1.call-update
  101.5 0.6 copy-done.3
  102.1 0.3 multiply_cosine_fusion
  102.4 0.0 all-gather.4.cloned.1.call-done
  102.4 49.6 %reduce-scatter.2.cloned.1.call-done = bf16[128,2048]{1,0:T(8,128)(2,1)} async-done(((bf16[1024,2048]{1,0:T(8,128)(2,1)}), bf16[128,2048]{1,0:T(8,128)(2,1)}) %reduce-scatter.2.cloned.1.call-update) | async-done | bytes 524304 | tf_op jit(solution)/shard_map/reduce_scatter | solution.py:109
  152.0 15.7 %fusion.15 = f32[16,8,16,128]{3,1,2,0:T(8,128)S(1)} fusion(bf16[128,8192]{1,0:T(8,128)(2,1)} %all-gather.4.cloned.1.call-done, bf16[8192,2048]{1,0:T(8,128)(2,1)} %param.10, bf16[128,2048]{1,0:T(8,128)(2,1)} %reduce-scatter.2.cloned.1.call-done), kind=kOutput, calls=%fused_computation.19 | convolution fusion | flops 4295491584 | bytes 37224448 | tf_op jit(solution)/shard_map/dot_general | solution.py:92
  167.7 0.2 copy.23
  167.9 0.5 subtract_convert_fusion
  168.4 0.3 pad_maximum_fusion
  168.7 0.2 broadcast_in_dim.55
  168.9 0.1 constant_dynamic-update-slice_fusion.2
  169.1 0.0 copy-start.2
  169.1 1.5 collective-permute-start
  170.6 1.5 collective-permute-start.1
  172.1 12.8 %collective-permute-done = bf16[128,2048]{1,0:T(8,128)(2,1)S(1)} collective-permute-done((bf16[128,2048]{1,0:T(8,128)(2,1)S(1)}, bf16[128,2048]{1,0:T(8,128)(2,1)S(1)}, u32[]{:S(2)}, u32[]{:S(2)}) %collective-permute-start) | collective-permute-done | bytes 524320 | tf_op jit(solution)/shard_map/ppermute | solution.py:20
  184.9 0.5 collective-permute-start.2
  185.4 0.1 broadcast_compare_fusion
  185.6 0.0 copy-start.1
  185.7 10.6 %collective-permute-done.1 = bf16[128,2048]{1,0:T(8,128)(2,1)} collective-permute-done((bf16[128,2048]{1,0:T(8,128)(2,1)S(1)}, bf16[128,2048]{1,0:T(8,128)(2,1)}, u32[]{:S(2)}, u32[]{:S(2)}) %collective-permute-start.1) | collective-permute-done | bytes 524320 | tf_op jit(solution)/shard_map/ppermute | solution.py:26
  196.2 1.1 constant_dynamic-update-slice_fusion
  197.3 6.8 %collective-permute-done.2 = bf16[128,2048]{1,0:T(8,128)(2,1)} collective-permute-done((bf16[128,2048]{1,0:T(8,128)(2,1)S(1)}, bf16[128,2048]{1,0:T(8,128)(2,1)}, u32[]{:S(2)}, u32[]{:S(2)}) %collective-permute-start.2) | collective-permute-done | bytes 524320 | tf_op jit(solution)/shard_map/ppermute | solution.py:20
  204.1 1.1 constant_dynamic-update-slice_fusion.3
  205.2 0.6 copy.25
  205.8 0.0 copy-done.1
  205.8 2.4 fusion
  208.2 0.0 copy-done.2
  208.2 0.0 copy-start
  208.2 1.9 copy-done
  210.1 3.1 %fusion.1 = f32[128,8,8]{2,1,0:T(8,128)S(1)} fusion(f32[128,8,8,16]{3,2,1,0:T(8,128)S(1)} %get-tuple-element.11, f32[128,8,8]{2,1,0:T(8,128)S(1)} %get-tuple-element.10, pred[128,16]{1,0:T(8,128)(4,1)S(1)} %broadcast_compare_fusion), kind=kLoop, calls=%fused_computation.7 | loop fusion | flops 647168 | bytes 591872 | tf_op jit(solution)/shard_map/reduce_sum | solution.py:130
  213.2 0.8 copy.21
  214.0 3.3 %all-to-all-start.2 = ((f32[128,4,16]{0,2,1:T(8,128)}), f32[128,4,16]{0,2,1:T(8,128)S(1)}, u32[]{:S(2)}, u32[]{:S(2)}) async-start(f32[128,4,16]{0,2,1:T(8,128)} %bitcast.7), calls=%async_computation.3 | async-start | bytes 65536 | tf_op jit(solution)/shard_map/all_to_all | solution.py:141
  217.3 0.8 copy.18
  218.1 3.9 %all-to-all-done.2 = f32[128,4,16]{0,2,1:T(8,128)S(1)} async-done(((f32[128,4,16]{0,2,1:T(8,128)}), f32[128,4,16]{0,2,1:T(8,128)S(1)}, u32[]{:S(2)}, u32[]{:S(2)}) %all-to-all-start.2) | async-done | bytes 32800 | tf_op jit(solution)/shard_map/all_to_all | solution.py:141
  222.0 3.3 %all-to-all-start = ((f32[128,4,16]{0,2,1:T(8,128)}), f32[128,4,16]{0,2,1:T(8,128)S(1)}, u32[]{:S(2)}, u32[]{:S(2)}) async-start(f32[128,4,16]{0,2,1:T(8,128)} %bitcast.6), calls=%async_computation.1 | async-start | bytes 65536 | tf_op jit(solution)/shard_map/all_to_all | solution.py:138
  225.3 6.4 %fusion.12 = bf16[128,8,8,128]{3,2,1,0:T(8,128)(2,1)} fusion(bf16[128,8,16,128]{3,2,1,0:T(8,128)(2,1)} %param.17, f32[128,8,8,16]{3,2,1,0:T(8,128)} %copy-done, f32[128,8,8]{2,1,0:T(8,128)S(1)} %get-tuple-element.10, pred[128,16]{1,0:T(8,128)(4,1)S(1)} %broadcast_compare_fusion), kind=kOutput, calls=%fused_computation.18 | convolution fusion | flops 35258368 | bytes 6850560 | tf_op jit(solution)/shard_map/rkgp,rkpd->rkgd/dot_general | solution.py:131
  231.7 2.5 reshape.175
  234.2 2.5 copy.20
  236.8 0.0 all-to-all-done
  236.8 4.2 %all-to-all-start.1 = ((bf16[128,4,2048]{2,0,1:T(8,128)(2,1)}), bf16[128,4,2048]{2,0,1:T(8,128)(2,1)S(1)}, u32[]{:S(2)}, u32[]{:S(2)}) async-start(bf16[128,4,2048]{2,0,1:T(8,128)(2,1)} %copy.20), calls=%async_computation.2 | async-start | bytes 4194304 | tf_op jit(solution)/shard_map/all_to_all | solution.py:145
  241.0 0.1 copy.19
  241.1 2.6 mul.135
  243.7 4.9 %mul.136 = f32[128,4,2048]{2,0,1:T(8,128)} reshape(f32[128,4,16,128]{3,2,0,1:T(8,128)} %mul.135) | data formatting | bytes 8388608 | tf_op jit(solution)/shard_map/mul | solution.py:151
  248.5 0.1 copy.22
  248.6 12.6 %all-to-all-done.1 = bf16[128,4,2048]{2,0,1:T(8,128)(2,1)S(1)} async-done(((bf16[128,4,2048]{2,0,1:T(8,128)(2,1)}), bf16[128,4,2048]{2,0,1:T(8,128)(2,1)S(1)}, u32[]{:S(2)}, u32[]{:S(2)}) %all-to-all-start.1) | async-done | bytes 2097184 | tf_op jit(solution)/shard_map/all_to_all | solution.py:145
  261.3 2.9 %multiply_reduce_fusion = f32[128,2048]{1,0:T(8,128)S(1)} fusion(f32[128,4,2048]{2,0,1:T(8,128)} %mul.136, bf16[128,4,2048]{2,0,1:T(8,128)(2,1)S(1)} %all-to-all-done.1), kind=kLoop, calls=%fused_computation.1 | loop fusion | flops 2883584 | bytes 7340032 | tf_op jit(solution)/shard_map/reduce_sum | solution.py:150
  264.2 0.3 div.27
  264.5 1.2 fusion.16
  (9 shorter events, 0.1 us)
Async XLA Ops:
  7.2 52.3 %all-gather.6.cloned.1.call-start = ((), (), s32[]{:S(2)}) async-start(), calls=%async_computation.5 | async-start | bytes 4718592 | tf_op jit(solution)/shard_map/all_gather | solution.py:98
  7.9 94.5 %all-gather.4.cloned.1.call-start = ((), (), s32[]{:S(2)}) async-start(), calls=%async_computation.4 | async-start | bytes 2621440 | tf_op jit(solution)/shard_map/all_gather | solution.py:93
  8.6 143.3 %reduce-scatter.2.cloned.1.call-start = ((), (), s32[]{:S(2)}) async-start(), calls=%async_computation.6 | async-start | bytes 4718592 | tf_op jit(solution)/shard_map/reduce_scatter | solution.py:109
  101.4 0.7 copy-start.3
  169.1 39.1 %copy-start.2 = (bf16[128,2048]{1,0:T(8,128)(2,1)}, bf16[128,2048]{1,0:T(8,128)(2,1)S(1)}, u32[]{:S(2)}) copy-start(bf16[128,2048]{1,0:T(8,128)(2,1)S(1)} %get-tuple-element.5) | copy-start | bytes 1572868
  169.1 15.8 %collective-permute-start = (bf16[128,2048]{1,0:T(8,128)(2,1)S(1)}, bf16[128,2048]{1,0:T(8,128)(2,1)S(1)}, u32[]{:S(2)}, u32[]{:S(2)}) collective-permute-start(bf16[128,2048]{1,0:T(8,128)(2,1)S(1)} %get-tuple-element.5), channel_id=1, source_target_pairs={{0,1},{1,2},{2,3},{3,0},{4,5},{5,6},{6,7},{7,4},{8,9},{9,10},{10,1... | collective-permute-start | bytes 1572872 | tf_op jit(solution)/shard_map/ppermute | solution.py:20
  170.6 25.7 %collective-permute-start.1 = (bf16[128,2048]{1,0:T(8,128)(2,1)S(1)}, bf16[128,2048]{1,0:T(8,128)(2,1)}, u32[]{:S(2)}, u32[]{:S(2)}) collective-permute-start(bf16[128,2048]{1,0:T(8,128)(2,1)S(1)} %get-tuple-element.5), channel_id=1, source_target_pairs={{0,3},{1,0},{2,1},{3,2},{4,7},{5,4},{6,5},{7,6},{8,11},{9,8},{10,9... | collective-permute-start | bytes 1572872 | tf_op jit(solution)/shard_map/ppermute | solution.py:26
  184.9 19.2 %collective-permute-start.2 = (bf16[128,2048]{1,0:T(8,128)(2,1)S(1)}, bf16[128,2048]{1,0:T(8,128)(2,1)}, u32[]{:S(2)}, u32[]{:S(2)}) collective-permute-start(bf16[128,2048]{1,0:T(8,128)(2,1)S(1)} %collective-permute-done), channel_id=1, source_target_pairs={{0,1},{1,2},{2,3},{3,0},{4,5},{5,6},{6,7},{7,4},{8,9},{9,10},{10,1... | collective-permute-start | bytes 1572872 | tf_op jit(solution)/shard_map/ppermute | solution.py:20
  185.6 20.2 %copy-start.1 = (bf16[128,8,16,128]{3,2,1,0:T(8,128)(2,1)S(1)}, bf16[128,8,16,128]{3,2,1,0:T(8,128)(2,1)}, u32[]{:S(2)}) copy-start(bf16[128,8,16,128]{3,2,1,0:T(8,128)(2,1)} %param.16) | copy-start | bytes 12582916
  208.2 1.9 copy-start
  214.0 8.0 %all-to-all-start.2 = ((f32[128,4,16]{0,2,1:T(8,128)}), f32[128,4,16]{0,2,1:T(8,128)S(1)}, u32[]{:S(2)}, u32[]{:S(2)}) async-start(f32[128,4,16]{0,2,1:T(8,128)} %bitcast.7), calls=%async_computation.3 | async-start | bytes 65536 | tf_op jit(solution)/shard_map/all_to_all | solution.py:141
  222.0 14.7 %all-to-all-start = ((f32[128,4,16]{0,2,1:T(8,128)}), f32[128,4,16]{0,2,1:T(8,128)S(1)}, u32[]{:S(2)}, u32[]{:S(2)}) async-start(f32[128,4,16]{0,2,1:T(8,128)} %bitcast.6), calls=%async_computation.1 | async-start | bytes 65536 | tf_op jit(solution)/shard_map/all_to_all | solution.py:138
  236.8 24.5 %all-to-all-start.1 = ((bf16[128,4,2048]{2,0,1:T(8,128)(2,1)}), bf16[128,4,2048]{2,0,1:T(8,128)(2,1)S(1)}, u32[]{:S(2)}, u32[]{:S(2)}) async-start(bf16[128,4,2048]{2,0,1:T(8,128)(2,1)} %copy.20), calls=%async_computation.2 | async-start | bytes 4194304 | tf_op jit(solution)/shard_map/all_to_all | solution.py:145
Sparse Core Ops, SparseCore 0:
  9.6 49.8 all-gather.5
  61.3 38.8 all-gather.3
  102.5 49.4 reduce-scatter.1
